TPU v7x, 256 devices: a whole 4x4x8 slice. The times are simulated.
256 devices in a mesh: frow: 16 (over z, x_lo), fcol: 16 (over y, x_hi, core).
Axes of the slice: x: 4 (x_hi: 2, x_lo: 2; x = x_hi * 2 + x_lo), y: 4, z: 8, core: 2. Of those that a mesh axis runs over, the one named last changes fastest.
Arguments:
- facets: float32 [2, 2048, 16384], P(None, 'frow', 'fcol'), may hold values from -6 to 6
- column_start: int32 [1], replicated, may hold values from 0 to 16383
- subgrid_start: int32 [16], replicated, may hold values from 0 to 2047
- vis_count: int32 [16], P('frow'), may hold values from 1 to 64
- vis_row: int32 [16, 64], P('frow'), may hold values from 0 to 511
- vis_weight: float32 [16, 64, 512], P('frow', None, 'fcol'), may hold values from -1 to 1
Outputs:
- corrected: float32 [16, 512, 2, 512], P('frow', 'fcol')
- facet_update: float32 [2, 2048, 16384], P(None, 'frow', 'fcol')
All inputs are finite; a program needn't handle non-finite values.
Results may differ from a plain program's by a relative error of at most 0.0003.
Values sent between devices are 32-bit elements; how exact they have to be, the bound alone decides.
A program may use at most 64 MiB of HBM per device.

v0:
```python
import math
import jax
import jax.numpy as jnp
from jax import lax
from jax.sharding import PartitionSpec as P

SG = 512
MAXB = 64
HIGH = lax.Precision.HIGHEST


def table(first, count, anchor, length, modulus):
    freqs = (first + jnp.arange(count, dtype=jnp.int32)) % modulus
    coords = anchor + jnp.arange(length, dtype=jnp.int32)
    phase = freqs[:, None] * coords[None, :] % modulus
    angle = phase.astype(jnp.float32) * jnp.float32(2.0 * math.pi / modulus)
    scale = jnp.float32(1.0 / math.sqrt(modulus))
    return (jnp.cos(angle) * scale, jnp.sin(angle) * scale)


def table_batch(firsts, anchors, count, length, modulus):
    freqs = (firsts[..., None] + jnp.arange(count, dtype=jnp.int32)) % modulus
    coords = anchors[..., None] + jnp.arange(length, dtype=jnp.int32)
    phase = freqs[..., :, None] * coords[..., None, :] % modulus
    angle = phase.astype(jnp.float32) * jnp.float32(2.0 * math.pi / modulus)
    scale = jnp.float32(1.0 / math.sqrt(modulus))
    return (jnp.cos(angle) * scale, jnp.sin(angle) * scale)


def contract(form, left, right):
    return jnp.einsum(form, left, right, precision=HIGH)


def per_device(facets, column_start, subgrid_start, vis_count, vis_row, vis_weight):
    row_index = lax.axis_index("frow")
    col_index = lax.axis_index("fcol")
    row_devices = lax.axis_size("frow")
    col_devices = lax.axis_size("fcol")
    height, width = (facets.shape[1], facets.shape[2])
    rows_total = height * row_devices
    cols_total = width * col_devices
    sub_owned = vis_count.shape[0]
    col_local = SG // col_devices
    real_part, imag_part = (facets[0], facets[1])
    col_cos, col_sin = table(
        column_start[0], col_local * lax.axis_size("fcol"), col_index * width, width, cols_total
    )
    strip_re = contract("qy,xy->qx", col_cos, real_part) + contract("qy,xy->qx", col_sin, imag_part)
    strip_im = contract("qy,xy->qx", col_cos, imag_part) - contract("qy,xy->qx", col_sin, real_part)
    strip = lax.psum_scatter(
        jnp.stack([strip_re, strip_im], 1), "fcol", scatter_dimension=0, tiled=True
    )
    anchors = jnp.zeros((sub_owned * lax.axis_size("frow"),), jnp.int32) + row_index * height
    row_cos, row_sin = table_batch(subgrid_start, anchors, SG, height, rows_total)
    sub_re = contract("qx,spx->sqp", strip[:, 0], row_cos) + contract(
        "qx,spx->sqp", strip[:, 1], row_sin
    )
    sub_im = contract("qx,spx->sqp", strip[:, 1], row_cos) - contract(
        "qx,spx->sqp", strip[:, 0], row_sin
    )
    subs = lax.psum_scatter(jnp.stack([sub_re, sub_im], 2), "frow", scatter_dimension=0, tiled=True)
    live = (jnp.arange(MAXB, dtype=jnp.int32)[None, :] < vis_count[:, None]).astype(jnp.float32)
    onehot = (vis_row[:, :, None] == jnp.arange(SG, dtype=jnp.int32)[None, None, :]).astype(
        jnp.float32
    )
    gain = 1.0 + contract("sbq,sbp->sqp", vis_weight * live[:, :, None], onehot)
    corrected = subs * gain[:, :, None, :]
    piece = lax.all_gather(corrected, "frow", axis=0, tiled=True)
    count = piece.shape[0]
    anchors = jnp.zeros((count,), jnp.int32) + row_index * height
    row_cos, row_sin = table_batch(subgrid_start, anchors, SG, height, rows_total)
    back_re = contract("mqp,mpx->qx", piece[:, :, 0], row_cos) - contract(
        "mqp,mpx->qx", piece[:, :, 1], row_sin
    )
    back_im = contract("mqp,mpx->qx", piece[:, :, 1], row_cos) + contract(
        "mqp,mpx->qx", piece[:, :, 0], row_sin
    )
    back = jnp.stack([back_re, back_im], 1)
    piece = lax.all_gather(back, "fcol", axis=0, tiled=True)
    col_cos, col_sin = table(column_start[0], piece.shape[0], col_index * width, width, cols_total)
    image_re = contract("qx,qy->xy", piece[:, 0], col_cos) - contract(
        "qx,qy->xy", piece[:, 1], col_sin
    )
    image_im = contract("qx,qy->xy", piece[:, 1], col_cos) + contract(
        "qx,qy->xy", piece[:, 0], col_sin
    )
    facet_update = jnp.stack([image_re, image_im])
    return (corrected, facet_update)


def solution(mesh):
    return jax.shard_map(
        per_device,
        mesh=mesh,
        in_specs=(
            P(None, "frow", "fcol"),
            P(),
            P(),
            P("frow"),
            P("frow", None),
            P("frow", None, "fcol"),
        ),
        out_specs=(P("frow", "fcol", None, None), P(None, "frow", "fcol")),
        check_vma=False,
    )
```

profile of v0, /device:TPU:1, one launch (start us, length us, event | category | flops | bytes accessed | tf_op | source)
XLA Modules:
  0.0 582.7 jit_solution(18072297512777448642)
XLA Ops:
  7.2 0.0 reduce-scatter.5.cloned.1.call-start
  7.9 10.5 %fusion.33 = f32[512,128]{1,0:T(8,128)S(1)} fusion(s32[1024]{0:T(1024)S(1)} %iota_add_fusion, s32[512]{0:T(512)S(1)} %add_select_fusion.3, f32[2,128,1024]{2,1,0:T(8,128)} %param.6), kind=kOutput, calls=%fused_computation.40 | convolution fusion | flops 813170688 | bytes 792576 | tf_op jit(solution)/shard_map/qy,xy->qx/dot_general | solution.py:31
  18.4 9.6 %fusion.32 = f32[512,128]{1,0:T(8,128)S(1)} fusion(s32[1024]{0:T(1024)S(1)} %iota_add_fusion, s32[512]{0:T(512)S(1)} %add_select_fusion.3, f32[2,128,1024]{2,1,0:T(8,128)S(1)} %copy-done.4), kind=kOutput, calls=%fused_computation.39 | convolution fusion | flops 813170688 | bytes 792576 | tf_op jit(solution)/shard_map/qy,xy->qx/dot_general | solution.py:31
  28.0 9.9 %fusion.47 = f32[512,1,128]{2,0,1:T(8,128)S(1)} fusion(f32[512,128]{1,0:T(8,128)S(1)} %fusion.33, s32[1024]{0:T(1024)S(1)} %iota_add_fusion, s32[512]{0:T(512)S(1)} %add_select_fusion.3, f32[2,128,1024]{2,1,0:T(8,128)S(1)} %copy-done.4), kind=kOutput, calls=%fused_computation.54 | convolution fusion | flops 813236224 | bytes 1054720 | tf_op jit(solution)/shard_map/qy,xy->qx/dot_general | solution.py:31
  37.9 9.6 %fusion.49 = f32[512,1,128]{2,0,1:T(8,128)S(1)} fusion(f32[512,128]{1,0:T(8,128)S(1)} %fusion.32, s32[1024]{0:T(1024)S(1)} %iota_add_fusion, s32[512]{0:T(512)S(1)} %add_select_fusion.3, f32[2,128,1024]{2,1,0:T(8,128)S(1)} %copy-done.4), kind=kOutput, calls=%fused_computation.56 | convolution fusion | flops 813236224 | bytes 1054720 | tf_op jit(solution)/shard_map/qy,xy->qx/dot_general | solution.py:31
  47.5 0.8 pad_maximum_fusion.2
  48.3 0.0 reduce-scatter.5.cloned.1.call-update
  48.3 0.0 all-reduce.3.cloned.1.call-start
  48.4 0.1 add_select_fusion.2
  48.5 75.3 %reduce-scatter.5.cloned.1.call-done = f32[32,2,128]{2,0,1:T(8,128)} async-done(((f32[512,2,128]{2,0,1:T(8,128)}), f32[32,2,128]{2,0,1:T(8,128)}) %reduce-scatter.5.cloned.1.call-update) | async-done | bytes 32784 | tf_op jit(solution)/shard_map/reduce_scatter | solution.py:50
  123.8 21.4 %fusion.6 = f32[16,512,32]{1,2,0:T(8,128)S(1)} fusion(s32[128]{0:T(128)S(1)} %iota_add_fusion.1, s32[16,512]{1,0:T(8,128)S(1)} %add_select_fusion.2, f32[32,2,128]{2,0,1:T(8,128)} %reduce-scatter.5.cloned.1.call-done), kind=kOutput, calls=%fused_computation.18 | convolution fusion | flops 418381824 | bytes 1098240 | tf_op jit(solution)/shard_map/qx,spx->sqp/dot_general | solution.py:31
  145.1 20.6 %fusion.5 = f32[16,512,32]{1,2,0:T(8,128)S(1)} fusion(s32[128]{0:T(128)S(1)} %iota_add_fusion.1, s32[16,512]{1,0:T(8,128)S(1)} %add_select_fusion.2, f32[32,2,128]{2,0,1:T(8,128)S(1)} %copy-done.5), kind=kOutput, calls=%fused_computation.17 | convolution fusion | flops 418381824 | bytes 1098240 | tf_op jit(solution)/shard_map/qx,spx->sqp/dot_general | solution.py:31
  165.7 20.8 %fusion.39 = f32[16,32,1,512]{3,1,0,2:T(8,128)S(1)} fusion(f32[16,512,32]{1,2,0:T(8,128)S(1)} %fusion.6, s32[128]{0:T(128)S(1)} %iota_add_fusion.1, s32[16,512]{1,0:T(8,128)S(1)} %add_select_fusion.2, f32[32,2,128]{2,0,1:T(8,128)S(1)} %copy-done.5), kind=kOutput, calls=%fused_computation.46 | convolution fusion | flops 418643968 | bytes 2146816 | tf_op jit(solution)/shard_map/qx,spx->sqp/dot_general | solution.py:31
  186.5 20.8 %fusion.41 = f32[16,32,1,512]{3,1,0,2:T(8,128)S(1)} fusion(f32[16,512,32]{1,2,0:T(8,128)S(1)} %fusion.5, s32[128]{0:T(128)S(1)} %iota_add_fusion.1, s32[16,512]{1,0:T(8,128)S(1)} %add_select_fusion.2, f32[32,2,128]{2,0,1:T(8,128)S(1)} %copy-done.5), kind=kOutput, calls=%fused_computation.48 | convolution fusion | flops 418643968 | bytes 2146816 | tf_op jit(solution)/shard_map/qx,spx->sqp/dot_general | solution.py:31
  207.3 1.5 pad_maximum_fusion
  208.9 0.3 all-gather.2.cloned.1.call-start
  209.8 0.6 dynamic-slice
  210.4 0.2 convolution_add_fusion
  210.6 136.5 %all-reduce.3.cloned.1.call-done = f32[16,32,2,512]{3,1,0,2:T(8,128)} async-done(((f32[16,32,2,512]{3,1,0,2:T(8,128)}), f32[16,32,2,512]{3,1,0,2:T(8,128)}) %all-reduce.3.cloned.1.call-update) | async-done | bytes 2097168
  347.1 2.2 dynamic-slice_multiply_fusion
  349.3 1.7 copy.10
  351.0 69.5 %all-gather.2.cloned.1.call-done = f32[16,32,2,512]{3,1,0,2:T(8,128)} async-done(((f32[1,32,2,512]{3,1,0,2:T(8,128)}), f32[16,32,2,512]{3,1,0,2:T(8,128)}) %all-gather.2.cloned.1.call-update) | async-done | bytes 2097168 | tf_op jit(solution)/shard_map/all_gather | solution.py:68
  420.5 22.2 %fusion.50 = f32[32,128]{1,0:T(8,128)S(1)} fusion(s32[128]{0:T(128)S(1)} %iota_add_fusion.1, s32[16,512]{1,0:T(8,128)S(1)} %add_select_fusion.2, f32[16,32,2,512]{3,1,0,2:T(8,128)} %all-gather.2.cloned.1.call-done), kind=kOutput, calls=%fused_computation.58 | convolution fusion | flops 418381824 | bytes 1098240 | tf_op jit(solution)/shard_map/mqp,mpx->qx/dot_general | solution.py:31
  442.7 19.3 %fusion.51 = f32[32,128]{1,0:T(8,128)S(1)} fusion(s32[128]{0:T(128)S(1)} %iota_add_fusion.1, s32[16,512]{1,0:T(8,128)S(1)} %add_select_fusion.2, f32[16,32,2,512]{3,1,0,2:T(8,128)S(1)} %copy-done.3), kind=kOutput, calls=%fused_computation.59 | convolution fusion | flops 418381824 | bytes 1098240 | tf_op jit(solution)/shard_map/mqp,mpx->qx/dot_general | solution.py:31
  462.0 19.2 %fusion.57 = f32[32,1,128]{2,0,1:T(8,128)S(1)} fusion(f32[32,128]{1,0:T(8,128)S(1)} %fusion.50, s32[128]{0:T(128)S(1)} %iota_add_fusion.1, s32[16,512]{1,0:T(8,128)S(1)} %add_select_fusion.2, f32[16,32,2,512]{3,1,0,2:T(8,128)S(1)} %copy-done.3), kind=kOutput, calls=%fused_computation.65 | convolution fusion | flops 418385920 | bytes 1114624 | tf_op jit(solution)/shard_map/mqp,mpx->qx/dot_general | solution.py:31
  481.1 19.2 %fusion.55 = f32[32,1,128]{2,0,1:T(8,128)S(1)} fusion(f32[32,128]{1,0:T(8,128)S(1)} %fusion.51, s32[128]{0:T(128)S(1)} %iota_add_fusion.1, s32[16,512]{1,0:T(8,128)S(1)} %add_select_fusion.2, f32[16,32,2,512]{3,1,0,2:T(8,128)S(1)} %copy-done.3), kind=kOutput, calls=%fused_computation.63 | convolution fusion | flops 418385920 | bytes 1114624 | tf_op jit(solution)/shard_map/mqp,mpx->qx/dot_general | solution.py:31
  500.3 37.8 %all_gather.7 = f32[512,2,128]{2,0,1:T(8,128)S(1)} all-gather(f32[32,2,128]{2,0,1:T(8,128)S(1)} %pad_maximum_fusion.3), channel_id=1, replica_groups=mesh['frow'=16,'fcol'=16] {'fcol'}, dimensions={0}, use_global_device_ids=true | all-gather | bytes 557056 | tf_op jit(solution)/shard_map/all_gather | solution.py:79
  538.1 9.0 %fusion.31 = f32[128,1024]{1,0:T(8,128)S(1)} fusion(s32[1024]{0:T(1024)S(1)} %iota_add_fusion, s32[512]{0:T(512)S(1)} %add_select_fusion.3, f32[512,2,128]{2,0,1:T(8,128)S(1)} %all_gather.7), kind=kOutput, calls=%fused_computation.38 | convolution fusion | flops 813170688 | bytes 792576 | tf_op jit(solution)/shard_map/qx,qy->xy/dot_general | solution.py:31
  547.1 9.2 %fusion.30 = f32[128,1024]{1,0:T(8,128)S(1)} fusion(s32[1024]{0:T(1024)S(1)} %iota_add_fusion, s32[512]{0:T(512)S(1)} %add_select_fusion.3, f32[512,2,128]{2,0,1:T(8,128)S(1)} %all_gather.7), kind=kOutput, calls=%fused_computation.37 | convolution fusion | flops 813170688 | bytes 792576 | tf_op jit(solution)/shard_map/qx,qy->xy/dot_general | solution.py:31
  556.3 9.3 %fusion.43 = f32[1,128,1024]{2,1,0:T(8,128)S(1)} fusion(f32[128,1024]{1,0:T(8,128)S(1)} %fusion.31, s32[1024]{0:T(1024)S(1)} %iota_add_fusion, s32[512]{0:T(512)S(1)} %add_select_fusion.3, f32[512,2,128]{2,0,1:T(8,128)S(1)} %all_gather.7), kind=kOutput, calls=%fused_computation.50 | convolution fusion | flops 813301760 | bytes 1316864 | tf_op jit(solution)/shard_map/qx,qy->xy/dot_general | solution.py:31
  565.6 9.1 %fusion.45 = f32[1,128,1024]{2,1,0:T(8,128)S(1)} fusion(f32[128,1024]{1,0:T(8,128)S(1)} %fusion.30, s32[1024]{0:T(1024)S(1)} %iota_add_fusion, s32[512]{0:T(512)S(1)} %add_select_fusion.3, f32[512,2,128]{2,0,1:T(8,128)S(1)} %all_gather.7), kind=kOutput, calls=%fused_computation.52 | convolution fusion | flops 813301760 | bytes 1316864 | tf_op jit(solution)/shard_map/qx,qy->xy/dot_general | solution.py:31
  574.7 1.1 pad_maximum_fusion.1
  (21 shorter events, 0.1 us)
Async XLA Ops:
  7.2 116.6 %reduce-scatter.5.cloned.1.call-start = ((), (), s32[]{:S(2)}) async-start(), calls=%async_computation.1 | async-start | bytes 557056 | tf_op jit(solution)/shard_map/reduce_scatter | solution.py:50
  7.9 10.5 %copy-start.4 = (f32[2,128,1024]{2,1,0:T(8,128)S(1)}, f32[2,128,1024]{2,1,0:T(8,128)}, u32[]{:S(2)}) copy-start(f32[2,128,1024]{2,1,0:T(8,128)} %param.6) | copy-start | bytes 3145732
  37.9 10.5 %copy-start.1 = (s32[16]{0:T(128)S(1)}, s32[16]{0:T(128)}, u32[]{:S(2)}) copy-start(s32[16]{0:T(128)} %param.8) | copy-start | bytes 196
  48.3 298.8 %all-reduce.3.cloned.1.call-start = ((), (), s32[]{:S(2)}) async-start(), calls=%async_computation.3 | async-start | bytes 4194304
  123.8 21.4 %copy-start.5 = (f32[32,2,128]{2,0,1:T(8,128)S(1)}, f32[32,2,128]{2,0,1:T(8,128)}, u32[]{:S(2)}) copy-start(f32[32,2,128]{2,0,1:T(8,128)} %reduce-scatter.5.cloned.1.call-done) | copy-start | bytes 98308
  208.8 0.9 copy-start.6
  208.8 1.5 copy-start
  208.8 1.5 copy-start.2
  208.9 211.7 %all-gather.2.cloned.1.call-start = ((), (), s32[]{:S(2)}) async-start(), calls=%async_computation.2 | async-start | bytes 2228224 | tf_op jit(solution)/shard_map/all_gather | solution.py:68
  420.5 22.2 %copy-start.3 = (f32[16,32,2,512]{3,1,0,2:T(8,128)S(1)}, f32[16,32,2,512]{3,1,0,2:T(8,128)}, u32[]{:S(2)}) copy-start(f32[16,32,2,512]{3,1,0,2:T(8,128)} %all-gather.2.cloned.1.call-done) | copy-start | bytes 6291460
Sparse Core Ops, SparseCore 0:
  48.5 75.2 reduce-scatter.4
  209.0 138.0 all-reduce.2
  349.5 71.0 all-gather.1
where the time goes:
time: 592 us; the launch traced here: 583 us
  waiting for transfers between devices  281 us (47%)
  matrix products  240 us (41%)
  blocking collectives  37.8 us (6%)
  between operations  15.7 us (3%)
    dot_general x17, matrix products, contract(): return jnp.einsum(form, left, right, precision=HIGH)  240 us
    unnamed x4, waiting for transfers between devices  137 us
    reduce_scatter x1, waiting for transfers between devices, per_device(): lax.psum_scatter(jnp.stack([strip_re, strip_im], 1), 'fcol', scatter_dime...  75.3 us
    all_gather x1, waiting for transfers between devices, per_device(): piece = lax.all_gather(corrected, 'frow', axis=0, tiled=True)  69.5 us
    all_gather x1, blocking collectives, per_device(): piece = lax.all_gather(back, 'fcol', axis=0, tiled=True)  37.8 us
  transfers between devices with their start and end apart: 3, of which 3 were waited for; matrix products, arithmetic and copies ran while one was open for 0% of the time, Pallas kernels for 0%

commit v1 on v0

--- a/solution.py
+++ b/solution.py
@@ -65,7 +65,9 @@
     )
     gain = 1.0 + contract("sbq,sbp->sqp", vis_weight * live[:, :, None], onehot)
     corrected = subs * gain[:, :, None, :]
-    piece = lax.all_gather(corrected, "frow", axis=0, tiled=True)
+    piece = jnp.concatenate(
+        lax.all_to_all(jnp.stack([corrected] * lax.axis_size("frow")), "frow", 0, 0), axis=0
+    )
     count = piece.shape[0]
     anchors = jnp.zeros((count,), jnp.int32) + row_index * height
     row_cos, row_sin = table_batch(subgrid_start, anchors, SG, height, rows_total)

time: 592 us -> 563 us (0.951)
  waiting for transfers between devices: 281 us -> 249 us
    all_gather x1 -> x0, waiting for transfers between devices: 69.5 us -> none  [per_device(): piece = lax.all_gather(corrected, 'frow', axis=0, tiled=True)]
    all_to_all x0 -> x1, waiting for transfers between devices: none -> 36.3 us  [per_device(): lax.all_to_all(jnp.stack([corrected] * lax.axis_size('frow')), 'frow', 0, 0)]
    unnamed x4 -> x3, waiting for transfers between devices: 137 us -> 137 us
  transfers between devices with their start and end apart: 3 -> 3, of which waited for: 3 -> 3; matrix products, arithmetic and copies ran while one was open for 0% -> 1% of each run, Pallas kernels for 0% -> 0%
where the time goes in v1:
time: 563 us; the launch traced here: 554 us
  waiting for transfers between devices  249 us (44%)
  matrix products  237 us (42%)
  blocking collectives  38.3 us (7%)
  between operations  15.8 us (3%)
  other arithmetic  6.67 us (1%)
    dot_general x17, matrix products, contract(): return jnp.einsum(form, left, right, precision=HIGH)  237 us
    unnamed x3, waiting for transfers between devices  137 us
    reduce_scatter x1, waiting for transfers between devices, per_device(): lax.psum_scatter(jnp.stack([strip_re, strip_im], 1), 'fcol', scatter_dime...  75.2 us
    all_gather x1, blocking collectives, per_device(): piece = lax.all_gather(back, 'fcol', axis=0, tiled=True)  38.3 us
    all_to_all x1, waiting for transfers between devices, per_device(): lax.all_to_all(jnp.stack([corrected] * lax.axis_size('frow')), 'frow', 0, 0)  36.3 us
  transfers between devices with their start and end apart: 3, of which 3 were waited for; matrix products, arithmetic and copies ran while one was open for 1% of the time, Pallas kernels for 0%

profile of v1, /device:TPU:1, one launch (start us, length us, event | category | flops | bytes accessed | tf_op | source)
XLA Modules:
  0.0 554.2 jit_solution(12539753904108720818)
XLA Ops:
  7.9 10.5 %fusion.32 = f32[512,128]{1,0:T(8,128)S(1)} fusion(s32[1024]{0:T(1024)S(1)} %iota_add_fusion, s32[512]{0:T(512)S(1)} %add_select_fusion.3, f32[2,128,1024]{2,1,0:T(8,128)} %param.6), kind=kOutput, calls=%fused_computation.40 | convolution fusion | flops 813170688 | bytes 792576 | tf_op jit(solution)/shard_map/qy,xy->qx/dot_general | solution.py:31
  18.4 9.6 %fusion.33 = f32[512,128]{1,0:T(8,128)S(1)} fusion(s32[1024]{0:T(1024)S(1)} %iota_add_fusion, s32[512]{0:T(512)S(1)} %add_select_fusion.3, f32[2,128,1024]{2,1,0:T(8,128)S(1)} %copy-done.3), kind=kOutput, calls=%fused_computation.41 | convolution fusion | flops 813170688 | bytes 792576 | tf_op jit(solution)/shard_map/qy,xy->qx/dot_general | solution.py:31
  28.0 9.8 %fusion.49 = f32[512,1,128]{2,0,1:T(8,128)S(1)} fusion(f32[512,128]{1,0:T(8,128)S(1)} %fusion.32, s32[1024]{0:T(1024)S(1)} %iota_add_fusion, s32[512]{0:T(512)S(1)} %add_select_fusion.3, f32[2,128,1024]{2,1,0:T(8,128)S(1)} %copy-done.3), kind=kOutput, calls=%fused_computation.57 | convolution fusion | flops 813236224 | bytes 1054720 | tf_op jit(solution)/shard_map/qy,xy->qx/dot_general | solution.py:31
  37.8 9.6 %fusion.47 = f32[512,1,128]{2,0,1:T(8,128)S(1)} fusion(f32[512,128]{1,0:T(8,128)S(1)} %fusion.33, s32[1024]{0:T(1024)S(1)} %iota_add_fusion, s32[512]{0:T(512)S(1)} %add_select_fusion.3, f32[2,128,1024]{2,1,0:T(8,128)S(1)} %copy-done.3), kind=kOutput, calls=%fused_computation.55 | convolution fusion | flops 813236224 | bytes 1054720 | tf_op jit(solution)/shard_map/qy,xy->qx/dot_general | solution.py:31
  47.5 0.8 pad_maximum_fusion.2
  48.4 0.1 add_select_fusion.2
  48.5 75.2 %reduce-scatter.5.cloned.1.call-done = f32[32,2,128]{2,0,1:T(8,128)} async-done(((f32[512,2,128]{2,0,1:T(8,128)}), f32[32,2,128]{2,0,1:T(8,128)}) %reduce-scatter.5.cloned.1.call-update) | async-done | bytes 32784 | tf_op jit(solution)/shard_map/reduce_scatter | solution.py:50
  123.7 21.4 %fusion.5 = f32[16,512,32]{1,2,0:T(8,128)S(1)} fusion(s32[128]{0:T(128)S(1)} %iota_add_fusion.1, s32[16,512]{1,0:T(8,128)S(1)} %add_select_fusion.2, f32[32,2,128]{2,0,1:T(8,128)} %reduce-scatter.5.cloned.1.call-done), kind=kOutput, calls=%fused_computation.17 | convolution fusion | flops 418381824 | bytes 1098240 | tf_op jit(solution)/shard_map/qx,spx->sqp/dot_general | solution.py:31
  145.1 20.6 %fusion.6 = f32[16,512,32]{1,2,0:T(8,128)S(1)} fusion(s32[128]{0:T(128)S(1)} %iota_add_fusion.1, s32[16,512]{1,0:T(8,128)S(1)} %add_select_fusion.2, f32[32,2,128]{2,0,1:T(8,128)S(1)} %copy-done.4), kind=kOutput, calls=%fused_computation.18 | convolution fusion | flops 418381824 | bytes 1098240 | tf_op jit(solution)/shard_map/qx,spx->sqp/dot_general | solution.py:31
  165.7 20.8 %fusion.41 = f32[16,32,1,512]{3,1,0,2:T(8,128)S(1)} fusion(f32[16,512,32]{1,2,0:T(8,128)S(1)} %fusion.5, s32[128]{0:T(128)S(1)} %iota_add_fusion.1, s32[16,512]{1,0:T(8,128)S(1)} %add_select_fusion.2, f32[32,2,128]{2,0,1:T(8,128)S(1)} %copy-done.4), kind=kOutput, calls=%fused_computation.49 | convolution fusion | flops 418643968 | bytes 2146816 | tf_op jit(solution)/shard_map/qx,spx->sqp/dot_general | solution.py:31
  186.5 20.8 %fusion.39 = f32[16,32,1,512]{3,1,0,2:T(8,128)S(1)} fusion(f32[16,512,32]{1,2,0:T(8,128)S(1)} %fusion.6, s32[128]{0:T(128)S(1)} %iota_add_fusion.1, s32[16,512]{1,0:T(8,128)S(1)} %add_select_fusion.2, f32[32,2,128]{2,0,1:T(8,128)S(1)} %copy-done.4), kind=kOutput, calls=%fused_computation.47 | convolution fusion | flops 418643968 | bytes 2146816 | tf_op jit(solution)/shard_map/qx,spx->sqp/dot_general | solution.py:31
  207.3 1.5 pad_maximum_fusion
  209.5 0.6 dynamic-slice
  210.1 0.2 convolution_add_fusion
  210.4 136.9 %all-reduce.3.cloned.1.call-done = f32[16,32,2,512]{3,1,0,2:T(8,128)} async-done(((f32[16,32,2,512]{3,1,0,2:T(8,128)}), f32[16,32,2,512]{3,1,0,2:T(8,128)}) %all-reduce.3.cloned.1.call-update) | async-done | bytes 2097168
  347.3 1.6 fusion.173
  348.8 1.6 stack.61
  350.4 4.9 all-to-all-start
  355.3 1.6 dynamic-slice_multiply_fusion
  356.8 0.8 copy.11
  357.6 36.3 %all-to-all-done = f32[16,1,32,2,512]{4,2,3,1,0:T(8,128)S(1)} async-done(((f32[16,1,32,2,512]{4,2,3,1,0:T(8,128)}), f32[16,1,32,2,512]{4,2,3,1,0:T(8,128)S(1)}, u32[]{:S(2)}, u32[]{:S(2)}) %all-to-all-start) | async-done | bytes 2097184 | tf_op jit(solution)/shard_map/all_to_all | solution.py:69
  393.9 0.2 copy.15
  394.1 19.3 %fusion.51 = f32[32,128]{1,0:T(8,128)S(1)} fusion(s32[128]{0:T(128)S(1)} %iota_add_fusion.1, s32[16,512]{1,0:T(8,128)S(1)} %add_select_fusion.2, f32[16,32,2,512]{3,1,0,2:T(8,128)S(1)} %bitcast.97), kind=kOutput, calls=%fused_computation.60 | convolution fusion | flops 418381824 | bytes 1098240 | tf_op jit(solution)/shard_map/mqp,mpx->qx/dot_general | solution.py:31
  413.4 19.3 %fusion.50 = f32[32,128]{1,0:T(8,128)S(1)} fusion(s32[128]{0:T(128)S(1)} %iota_add_fusion.1, s32[16,512]{1,0:T(8,128)S(1)} %add_select_fusion.2, f32[16,32,2,512]{3,1,0,2:T(8,128)S(1)} %bitcast.98), kind=kOutput, calls=%fused_computation.59 | convolution fusion | flops 418381824 | bytes 1098240 | tf_op jit(solution)/shard_map/mqp,mpx->qx/dot_general | solution.py:31
  432.7 19.2 %fusion.55 = f32[32,1,128]{2,0,1:T(8,128)S(1)} fusion(f32[32,128]{1,0:T(8,128)S(1)} %fusion.51, s32[128]{0:T(128)S(1)} %iota_add_fusion.1, s32[16,512]{1,0:T(8,128)S(1)} %add_select_fusion.2, f32[16,32,2,512]{3,1,0,2:T(8,128)S(1)} %bitcast.99), kind=kOutput, calls=%fused_computation.64 | convolution fusion | flops 418385920 | bytes 1114624 | tf_op jit(solution)/shard_map/mqp,mpx->qx/dot_general | solution.py:31
  451.8 19.2 %fusion.57 = f32[32,1,128]{2,0,1:T(8,128)S(1)} fusion(f32[32,128]{1,0:T(8,128)S(1)} %fusion.50, s32[128]{0:T(128)S(1)} %iota_add_fusion.1, s32[16,512]{1,0:T(8,128)S(1)} %add_select_fusion.2, f32[16,32,2,512]{3,1,0,2:T(8,128)S(1)} %bitcast.100), kind=kOutput, calls=%fused_computation.66 | convolution fusion | flops 418385920 | bytes 1114624 | tf_op jit(solution)/shard_map/mqp,mpx->qx/dot_general | solution.py:31
  471.0 38.3 %all_gather.3 = f32[512,2,128]{2,0,1:T(8,128)S(1)} all-gather(f32[32,2,128]{2,0,1:T(8,128)S(1)} %pad_maximum_fusion.3), channel_id=1, replica_groups=mesh['frow'=16,'fcol'=16] {'fcol'}, dimensions={0}, use_global_device_ids=true | all-gather | bytes 557056 | tf_op jit(solution)/shard_map/all_gather | solution.py:81
  509.4 9.0 %fusion.30 = f32[128,1024]{1,0:T(8,128)S(1)} fusion(s32[1024]{0:T(1024)S(1)} %iota_add_fusion, s32[512]{0:T(512)S(1)} %add_select_fusion.3, f32[512,2,128]{2,0,1:T(8,128)S(1)} %all_gather.3), kind=kOutput, calls=%fused_computation.38 | convolution fusion | flops 813170688 | bytes 792576 | tf_op jit(solution)/shard_map/qx,qy->xy/dot_general | solution.py:31
  518.4 9.4 %fusion.31 = f32[128,1024]{1,0:T(8,128)S(1)} fusion(s32[1024]{0:T(1024)S(1)} %iota_add_fusion, s32[512]{0:T(512)S(1)} %add_select_fusion.3, f32[512,2,128]{2,0,1:T(8,128)S(1)} %all_gather.3), kind=kOutput, calls=%fused_computation.39 | convolution fusion | flops 813170688 | bytes 792576 | tf_op jit(solution)/shard_map/qx,qy->xy/dot_general | solution.py:31
  527.8 9.2 %fusion.45 = f32[1,128,1024]{2,1,0:T(8,128)S(1)} fusion(f32[128,1024]{1,0:T(8,128)S(1)} %fusion.30, s32[1024]{0:T(1024)S(1)} %iota_add_fusion, s32[512]{0:T(512)S(1)} %add_select_fusion.3, f32[512,2,128]{2,0,1:T(8,128)S(1)} %all_gather.3), kind=kOutput, calls=%fused_computation.53 | convolution fusion | flops 813301760 | bytes 1316864 | tf_op jit(solution)/shard_map/qx,qy->xy/dot_general | solution.py:31
  537.0 9.1 %fusion.43 = f32[1,128,1024]{2,1,0:T(8,128)S(1)} fusion(f32[128,1024]{1,0:T(8,128)S(1)} %fusion.31, s32[1024]{0:T(1024)S(1)} %iota_add_fusion, s32[512]{0:T(512)S(1)} %add_select_fusion.3, f32[512,2,128]{2,0,1:T(8,128)S(1)} %all_gather.3), kind=kOutput, calls=%fused_computation.51 | convolution fusion | flops 813301760 | bytes 1316864 | tf_op jit(solution)/shard_map/qx,qy->xy/dot_general | solution.py:31
  546.1 1.1 pad_maximum_fusion.1
  (21 shorter events, 0.2 us)
Async XLA Ops:
  7.2 116.6 %reduce-scatter.5.cloned.1.call-start = ((), (), s32[]{:S(2)}) async-start(), calls=%async_computation.2 | async-start | bytes 557056 | tf_op jit(solution)/shard_map/reduce_scatter | solution.py:50
  7.9 10.5 %copy-start.3 = (f32[2,128,1024]{2,1,0:T(8,128)S(1)}, f32[2,128,1024]{2,1,0:T(8,128)}, u32[]{:S(2)}) copy-start(f32[2,128,1024]{2,1,0:T(8,128)} %param.6) | copy-start | bytes 3145732
  37.8 10.6 %copy-start.1 = (s32[16]{0:T(128)S(1)}, s32[16]{0:T(128)}, u32[]{:S(2)}) copy-start(s32[16]{0:T(128)} %param.8) | copy-start | bytes 196
  48.3 298.9 %all-reduce.3.cloned.1.call-start = ((), (), s32[]{:S(2)}) async-start(), calls=%async_computation.3 | async-start | bytes 4194304
  123.7 21.4 %copy-start.4 = (f32[32,2,128]{2,0,1:T(8,128)S(1)}, f32[32,2,128]{2,0,1:T(8,128)}, u32[]{:S(2)}) copy-start(f32[32,2,128]{2,0,1:T(8,128)} %reduce-scatter.5.cloned.1.call-done) | copy-start | bytes 98308
  208.8 0.7 copy-start.5
  208.8 1.3 copy-start
  208.8 1.3 copy-start.2
  350.4 43.5 %all-to-all-start = ((f32[16,1,32,2,512]{4,2,3,1,0:T(8,128)}), f32[16,1,32,2,512]{4,2,3,1,0:T(8,128)S(1)}, u32[]{:S(2)}, u32[]{:S(2)}) async-start(f32[16,1,32,2,512]{4,2,3,1,0:T(8,128)} %stack.61), calls=%async_computation.1 | async-start | bytes 4194304 | tf_op jit(solution)/shard_map/all_to_all | solution.py:69
Sparse Core Ops, SparseCore 0:
  48.5 75.2 reduce-scatter.4
  209.0 138.2 all-reduce.2
